TPU v7x, 32 devices: a whole 2x2x4 slice. The times are simulated.
32 devices in a mesh: gx: 8 (over z, x), gy: 4 (over y, core).
Axes of the slice: x: 2, y: 2, z: 4, core: 2. Of those that a mesh axis runs over, the one named last changes fastest.
Arguments:
- site_frac: float32 [3, 16, 8, 128], P(None, 'gx', 'gy'), may hold values from 0 to 1
- dual_weight: float32 [16, 8, 128], P('gx', 'gy'), may hold values from -2.5 to 64
- target_mass: float32 [16, 8, 128], P('gx', 'gy'), may hold values from 0.2 to 0.8
- block_list: int32 [8, 4, 12], P('gx', 'gy'), may hold values from 0 to 35, as said below
- block_count: int32 [8, 4], P('gx', 'gy'), may hold values from 1 to 12, as said below
Outputs:
- new_dual: float32 [16, 8, 128], P('gx', 'gy')
- site_shift: float32 [3, 16, 8, 128], P(None, 'gx', 'gy')
- displacement: float32 [3, 32, 16, 256], P(None, 'gx', 'gy')
Inputs may be any that keep to these rules, and one draw needn't show every extreme that they name: `block_list`: within one tile the 12 entries are distinct. The first block_count entries name halo slots whose blocks hold sites of that tile's neighbourhood. `block_count`: some tile uses all 12 entries.
All inputs are finite; a program needn't handle non-finite values.
Results may differ from a plain program's by a relative error of at most 0.0003.
Values sent between devices are 32-bit elements; how exact they have to be, the bound alone decides.
A program may use at most 64 MiB of HBM per device.

v0:
```python
import math

import jax
import jax.numpy as jnp
from jax import lax
from jax.sharding import PartitionSpec as P

TX = 4
TY = 4
Z = 256


entropy_scale = 0.5
step_rate = 0.5


def with_halo(block, sides, width):
    for axis, dim in sides:
        count = lax.axis_size(axis)
        forward = [(i, i + 1) for i in range(count - 1)]
        forward.append((count - 1, 0))
        backward = [(target, source) for source, target in forward]
        low = lax.ppermute(
            lax.slice_in_dim(block, block.shape[dim] - width, None, axis=dim), axis, forward
        )
        high = lax.ppermute(lax.slice_in_dim(block, 0, width, axis=dim), axis, backward)
        block = jnp.concatenate([low, block, high], axis=dim)
    return block


def from_behind(shard, axis, by):
    peers = lax.axis_size(axis)
    return lax.ppermute(shard, axis, [(i, (i + by) % peers) for i in range(peers)])


def grid_points(first_row, how_many):
    serial = first_row + jnp.arange(how_many)
    cell_x = serial // (TY * Z)
    cell_y = serial // Z % TY
    cell_z = serial % Z
    return jnp.stack([cell_x, cell_y, cell_z]).astype(jnp.float32) + 0.5


def assign(points, chosen, usable, moments):
    spread = points[:, :, None] - chosen[:3, None, :]
    distance = spread[0] * spread[0] + spread[1] * spread[1] + spread[2] * spread[2]
    scores = jnp.where(usable[None, :], (chosen[3][None, :] - distance) / entropy_scale, -jnp.inf)
    peak_score = jnp.max(scores, axis=1, keepdims=True)
    weights = jnp.exp(scores - peak_score)
    shares = weights / jnp.sum(weights, axis=1, keepdims=True)
    masses = jnp.sum(shares, axis=0)
    if not moments:
        return (masses, None, None)
    moment = jnp.sum(shares[None] * spread, axis=1)
    offsets = -jnp.sum(shares[None] * spread, axis=2)
    return (masses, moment, offsets)


def sweep_rows(chosen, usable, moments):
    total_rows = TX * TY * Z
    block_rows = math.gcd(total_rows, 512)
    columns = chosen.shape[1]

    def visit_rows(totals, first_row):
        masses, moment, offsets = assign(
            grid_points(first_row, block_rows), chosen, usable, moments
        )
        if moments:
            return ((totals[0] + masses, totals[1] + moment), offsets)
        return ((totals[0] + masses, totals[1]), offsets)

    start_totals = (jnp.zeros((columns,), jnp.float32), jnp.zeros((3, columns), jnp.float32))
    (masses, moment), gathered = lax.scan(
        visit_rows, start_totals, jnp.arange(0, total_rows, block_rows)
    )
    if not moments:
        return (masses, moment, None)
    return (masses, moment, gathered.transpose(1, 0, 2).reshape(3, total_rows))


def site_stack(site_frac, duals):
    scaling = jnp.array([TX, TY, Z], jnp.float32)
    coords = site_frac * scaling[:, None, None, None]
    return jnp.concatenate([coords, duals[None]], 0)


def place_sites(stacked, per_side):
    offset = (jnp.arange(3 * per_side) // per_side - 1).astype(jnp.float32)
    return jnp.stack(
        [
            stacked[0] + offset[:, None, None] * TX,
            stacked[1] + offset[None, :, None] * TY,
            stacked[2],
            stacked[3],
        ]
    )


def neighbours(stacked, per_side):
    return with_halo(stacked, (("gx", 1), ("gy", 2)), per_side)


def fold_x(spread, per_side):
    lower_rim = spread[:, :per_side]
    middle = spread[:, per_side : 2 * per_side]
    upper_rim = spread[:, 2 * per_side :]
    from_above = from_behind(lower_rim, "gx", -1)
    from_below = from_behind(upper_rim, "gx", 1)
    return middle + from_above + from_below


def fold_y(spread, per_side):
    lower_rim = spread[:, :, :per_side]
    middle = spread[:, :, per_side : 2 * per_side]
    upper_rim = spread[:, :, 2 * per_side :]
    from_above = from_behind(lower_rim, "gy", -1)
    from_below = from_behind(upper_rim, "gy", 1)
    return middle + from_above + from_below


def on_device(site_frac, dual_weight, target_mass, block_list, block_count):
    per_side = site_frac.shape[1]
    block_size = site_frac.shape[3]
    chosen_ids = block_list[0, 0]
    slot_count = chosen_ids.shape[0]
    live_count = block_count[0, 0]
    usable = jnp.arange(slot_count * block_size) // block_size < live_count
    used_blocks = jnp.arange(slot_count) < live_count
    table_size = 9 * per_side * per_side
    placer = (
        (chosen_ids[:, None] == jnp.arange(table_size)[None, :]) & used_blocks[:, None]
    ).astype(jnp.float32)

    def one_step(surround, moments):
        flat_table = surround.reshape(4, table_size, block_size)
        chosen = flat_table[:, chosen_ids].reshape(4, slot_count * block_size)
        masses, moment, offsets = sweep_rows(chosen, usable, moments)
        if moments:
            partials = jnp.concatenate([masses[None], moment], 0)
        else:
            partials = masses[None]
        partials = partials.reshape(-1, slot_count, block_size)
        spread = jnp.einsum("ckb,kt->ctb", partials, placer, precision=lax.Precision.HIGHEST)
        spread = spread.reshape(-1, 3 * per_side, 3 * per_side, block_size)
        folded = fold_y(fold_x(spread, per_side), per_side)
        return (folded, offsets)

    surround = place_sites(neighbours(site_stack(site_frac, dual_weight), per_side), per_side)
    folded, ignored = one_step(surround, False)
    dual_mid = dual_weight + step_rate * (target_mass - folded[0])
    new_duals = with_halo(dual_mid[None], (("gx", 1), ("gy", 2)), per_side)
    surround = jnp.concatenate([surround[:3], new_duals], 0)
    folded, offsets = one_step(surround, True)
    new_dual = dual_mid + step_rate * (target_mass - folded[0])
    site_shift = folded[1:] / (folded[0] + target_mass)[None]
    displacement = offsets.reshape(3, TX, TY, Z)
    return (new_dual, site_shift, displacement)


def solution(mesh):
    in_specs = (
        P(None, "gx", "gy", None),
        P("gx", "gy", None),
        P("gx", "gy", None),
        P("gx", "gy", None),
        P("gx", "gy"),
    )
    out_specs = (P("gx", "gy", None), P(None, "gx", "gy", None), P(None, "gx", "gy", None))
    return jax.shard_map(
        on_device, mesh=mesh, in_specs=in_specs, out_specs=out_specs, check_vma=False
    )
```

profile of v0, /device:TPU:0, one launch (start us, length us, event | category | flops | bytes accessed | tf_op | source)
XLA Modules:
  0.0 177.3 jit_solution(18293934567586156023)
XLA Ops:
  2.1 3.0 %collective-permute-start = (f32[4,2,2,128]{3,2,1,0:T(2,128)S(1)}, f32[4,2,2,128]{3,2,1,0:T(2,128)S(1)}, u32[]{:S(2)}, u32[]{:S(2)}) collective-permute-start(f32[4,2,2,128]{3,2,1,0:T(2,128)S(1)} %pad_maximum_fusion.8), channel_id=1, source_target_pairs={{0,4},{4,8},{8,12},{12,16},{16,20},{20,24},{24,28},{28,0},{1,5},{5... | collective-permute-start | bytes 24584 | tf_op jit(solution)/shard_map/ppermute | solution.py:23
  5.1 3.1 %collective-permute-start.1 = (f32[4,2,2,128]{3,2,1,0:T(2,128)S(1)}, f32[4,2,2,128]{3,2,1,0:T(2,128)S(1)}, u32[]{:S(2)}, u32[]{:S(2)}) collective-permute-start(f32[4,2,2,128]{3,2,1,0:T(2,128)S(1)} %pad_maximum_fusion.8), channel_id=1, source_target_pairs={{4,0},{8,4},{12,8},{16,12},{20,16},{24,20},{28,24},{0,28},{5,1},{9... | collective-permute-start | bytes 24584 | tf_op jit(solution)/shard_map/ppermute | solution.py:26
  10.5 1.7 collective-permute-start.3
  12.2 1.5 collective-permute-done.2
  15.3 48.1 %while.32 = (s32[]{:T(128)}, f32[1536]{0:T(1024)S(1)}, f32[4,1536]{1,0:T(4,128)S(1)}, s32[8]{0:T(128)S(1)}, s32[]{:T(128)}, /*index=5*/s32[]{:T(128)}, s32[]{:T(128)}) while((s32[]{:T(128)}, f32[1536]{0:T(1024)S(1)}, f32[4,1536]{1,0:T(4,128)S(1)}, s32[8]{0:T(128)S(1)}, s32[]{:T(128)}, /*index=5*/s32[]{:T(128)}, s32[]{:T(128)}) %tuple.94), condition=%wide.region_4.5_spmd.clone, body=%wide.region_0.4_spmd.clone.sunk | while | flops 13413891 | bytes 28410988 | solution.py:73
  18.6 1.3 fusion.79
  24.7 1.3 fusion.79
  30.7 1.3 fusion.79
  36.7 1.3 fusion.79
  42.7 1.3 fusion.79
  48.7 1.3 fusion.79
  63.6 4.8 %collective-permute-start.4 = (f32[1,2,6,128]{3,2,1,0:T(8,128)S(1)}, f32[1,2,6,128]{3,2,1,0:T(8,128)S(1)}, u32[]{:S(2)}, u32[]{:S(2)}) collective-permute-start(f32[1,2,6,128]{3,2,1,0:T(8,128)S(1)} %get-tuple-element.324), channel_id=1, source_target_pairs={{0,28},{4,0},{8,4},{12,8},{16,12},{20,16},{24,20},{28,24},{1,29},{... | collective-permute-start | bytes 18440 | tf_op jit(solution)/shard_map/ppermute | solution.py:33
  68.4 1.4 collective-permute-done.4
  69.8 5.0 %collective-permute-done.5 = f32[1,2,6,128]{3,2,1,0:T(8,128)S(1)} collective-permute-done((f32[1,2,6,128]{3,2,1,0:T(8,128)S(1)}, f32[1,2,6,128]{3,2,1,0:T(8,128)S(1)}, u32[]{:S(2)}, u32[]{:S(2)}) %collective-permute-start.5) | collective-permute-done | bytes 6176 | tf_op jit(solution)/shard_map/ppermute | solution.py:33
  76.5 1.7 collective-permute-done.7
  78.2 4.7 %collective-permute-start.9 = (f32[1,2,2,128]{3,2,1,0:T(2,128)S(1)}, f32[1,2,2,128]{3,2,1,0:T(2,128)S(1)}, u32[]{:S(2)}, u32[]{:S(2)}) collective-permute-start(f32[1,2,2,128]{3,2,1,0:T(2,128)S(1)} %bitcast.108), channel_id=1, source_target_pairs={{4,0},{8,4},{12,8},{16,12},{20,16},{24,20},{28,24},{0,28},{5,1},{9... | collective-permute-start | bytes 6152 | tf_op jit(solution)/shard_map/ppermute | solution.py:26
  82.9 1.6 collective-permute-done.8
  84.6 1.7 collective-permute-start.11
  86.3 1.3 collective-permute-done.10
  88.3 72.6 %while.33 = (s32[]{:T(128)}, f32[1536]{0:T(1024)S(1)}, f32[3,1536]{1,0:T(4,128)S(1)}, f32[8,3,512]{2,1,0:T(4,128)S(1)}, f32[4,1536]{1,0:T(4,128)S(1)}, /*index=5*/s32[8]{0:T(128)S(1)}, s32[]{:T(128)}, s32[]{:T(128)}, s32[]{:T(128)}) while((s32[]{:T(128)}, f32[1536]{0:T(1024)S(1)}, f32[3,1536]{1,0:T(4,128)S(1)}, ...), condition=%wide.region_11.12_spmd.clone, body=%wide.region_5.11_spmd.clone.sunk | while | flops 31506432 | bytes 37996160 | solution.py:73
  94.5 1.9 %multiply_reduce_fusion.3 = (f32[3,512]{1,0:T(4,128)S(1)}, f32[3,1536]{1,0:T(4,128)S(1)}) fusion(f32[512,1536]{1,0:T(8,128)S(1)} %divide_bitcast_fusion.2, f32[3,1536]{1,0:T(4,128)S(1)} %bitcast.95, f32[3,512]{1,0:T(4,128)S(1)} %fusion.82), kind=kLoop, calls=%fused_computation.44.clone.1 | loop fusion | flops 9431040 | bytes 3194880 | tf_op jit(solution)/shard_map/while/body/eval_jaxpr/reduce_sum | solution.py:55
  103.6 1.9 %multiply_reduce_fusion.3 = (f32[3,512]{1,0:T(4,128)S(1)}, f32[3,1536]{1,0:T(4,128)S(1)}) fusion(f32[512,1536]{1,0:T(8,128)S(1)} %divide_bitcast_fusion.2, f32[3,1536]{1,0:T(4,128)S(1)} %bitcast.95, f32[3,512]{1,0:T(4,128)S(1)} %fusion.82), kind=kLoop, calls=%fused_computation.44.clone.1 | loop fusion | flops 9431040 | bytes 3194880 | tf_op jit(solution)/shard_map/while/body/eval_jaxpr/reduce_sum | solution.py:55
  112.7 1.9 %multiply_reduce_fusion.3 = (f32[3,512]{1,0:T(4,128)S(1)}, f32[3,1536]{1,0:T(4,128)S(1)}) fusion(f32[512,1536]{1,0:T(8,128)S(1)} %divide_bitcast_fusion.2, f32[3,1536]{1,0:T(4,128)S(1)} %bitcast.95, f32[3,512]{1,0:T(4,128)S(1)} %fusion.82), kind=kLoop, calls=%fused_computation.44.clone.1 | loop fusion | flops 9431040 | bytes 3194880 | tf_op jit(solution)/shard_map/while/body/eval_jaxpr/reduce_sum | solution.py:55
  121.8 1.9 %multiply_reduce_fusion.3 = (f32[3,512]{1,0:T(4,128)S(1)}, f32[3,1536]{1,0:T(4,128)S(1)}) fusion(f32[512,1536]{1,0:T(8,128)S(1)} %divide_bitcast_fusion.2, f32[3,1536]{1,0:T(4,128)S(1)} %bitcast.95, f32[3,512]{1,0:T(4,128)S(1)} %fusion.82), kind=kLoop, calls=%fused_computation.44.clone.1 | loop fusion | flops 9431040 | bytes 3194880 | tf_op jit(solution)/shard_map/while/body/eval_jaxpr/reduce_sum | solution.py:55
  130.8 1.9 %multiply_reduce_fusion.3 = (f32[3,512]{1,0:T(4,128)S(1)}, f32[3,1536]{1,0:T(4,128)S(1)}) fusion(f32[512,1536]{1,0:T(8,128)S(1)} %divide_bitcast_fusion.2, f32[3,1536]{1,0:T(4,128)S(1)} %bitcast.95, f32[3,512]{1,0:T(4,128)S(1)} %fusion.82), kind=kLoop, calls=%fused_computation.44.clone.1 | loop fusion | flops 9431040 | bytes 3194880 | tf_op jit(solution)/shard_map/while/body/eval_jaxpr/reduce_sum | solution.py:55
  139.9 1.9 %multiply_reduce_fusion.3 = (f32[3,512]{1,0:T(4,128)S(1)}, f32[3,1536]{1,0:T(4,128)S(1)}) fusion(f32[512,1536]{1,0:T(8,128)S(1)} %divide_bitcast_fusion.2, f32[3,1536]{1,0:T(4,128)S(1)} %bitcast.95, f32[3,512]{1,0:T(4,128)S(1)} %fusion.82), kind=kLoop, calls=%fused_computation.44.clone.1 | loop fusion | flops 9431040 | bytes 3194880 | tf_op jit(solution)/shard_map/while/body/eval_jaxpr/reduce_sum | solution.py:55
  149.0 1.9 %multiply_reduce_fusion.3 = (f32[3,512]{1,0:T(4,128)S(1)}, f32[3,1536]{1,0:T(4,128)S(1)}) fusion(f32[512,1536]{1,0:T(8,128)S(1)} %divide_bitcast_fusion.2, f32[3,1536]{1,0:T(4,128)S(1)} %bitcast.95, f32[3,512]{1,0:T(4,128)S(1)} %fusion.82), kind=kLoop, calls=%fused_computation.44.clone.1 | loop fusion | flops 9431040 | bytes 3194880 | tf_op jit(solution)/shard_map/while/body/eval_jaxpr/reduce_sum | solution.py:55
  158.1 1.9 %multiply_reduce_fusion.3 = (f32[3,512]{1,0:T(4,128)S(1)}, f32[3,1536]{1,0:T(4,128)S(1)}) fusion(f32[512,1536]{1,0:T(8,128)S(1)} %divide_bitcast_fusion.2, f32[3,1536]{1,0:T(4,128)S(1)} %bitcast.95, f32[3,512]{1,0:T(4,128)S(1)} %fusion.82), kind=kLoop, calls=%fused_computation.44.clone.1 | loop fusion | flops 9431040 | bytes 3194880 | tf_op jit(solution)/shard_map/while/body/eval_jaxpr/reduce_sum | solution.py:55
  161.3 4.7 %collective-permute-start.12 = (f32[4,2,6,128]{3,2,1,0:T(8,128)S(1)}, f32[4,2,6,128]{3,2,1,0:T(8,128)S(1)}, u32[]{:S(2)}, u32[]{:S(2)}) collective-permute-start(f32[4,2,6,128]{3,2,1,0:T(8,128)S(1)} %copy.25), channel_id=1, source_target_pairs={{0,28},{4,0},{8,4},{12,8},{16,12},{20,16},{24,20},{28,24},{1,29},{... | collective-permute-start | bytes 73736 | tf_op jit(solution)/shard_map/ppermute | solution.py:33
  166.0 1.6 collective-permute-done.12
  167.6 5.0 %collective-permute-done.13 = f32[4,2,6,128]{3,2,1,0:T(8,128)S(1)} collective-permute-done((f32[4,2,6,128]{3,2,1,0:T(8,128)S(1)}, f32[4,2,6,128]{3,2,1,0:T(8,128)S(1)}, u32[]{:S(2)}, u32[]{:S(2)}) %collective-permute-start.13) | collective-permute-done | bytes 24608 | tf_op jit(solution)/shard_map/ppermute | solution.py:33
  174.4 1.7 collective-permute-done.15
  (258 shorter events, 107.5 us)
Async XLA Ops:
  2.1 7.6 %collective-permute-start = (f32[4,2,2,128]{3,2,1,0:T(2,128)S(1)}, f32[4,2,2,128]{3,2,1,0:T(2,128)S(1)}, u32[]{:S(2)}, u32[]{:S(2)}) collective-permute-start(f32[4,2,2,128]{3,2,1,0:T(2,128)S(1)} %pad_maximum_fusion.8), channel_id=1, source_target_pairs={{0,4},{4,8},{8,12},{12,16},{16,20},{20,24},{24,28},{28,0},{1,5},{5... | collective-permute-start | bytes 24584 | tf_op jit(solution)/shard_map/ppermute | solution.py:23
  5.1 4.7 %collective-permute-start.1 = (f32[4,2,2,128]{3,2,1,0:T(2,128)S(1)}, f32[4,2,2,128]{3,2,1,0:T(2,128)S(1)}, u32[]{:S(2)}, u32[]{:S(2)}) collective-permute-start(f32[4,2,2,128]{3,2,1,0:T(2,128)S(1)} %pad_maximum_fusion.8), channel_id=1, source_target_pairs={{4,0},{8,4},{12,8},{16,12},{20,16},{24,20},{28,24},{0,28},{5,1},{9... | collective-permute-start | bytes 24584 | tf_op jit(solution)/shard_map/ppermute | solution.py:26
  10.4 3.3 %collective-permute-start.2 = (f32[4,6,2,128]{3,2,1,0:T(2,128)S(1)}, f32[4,6,2,128]{3,2,1,0:T(2,128)S(1)}, u32[]{:S(2)}, u32[]{:S(2)}) collective-permute-start(f32[4,6,2,128]{3,2,1,0:T(2,128)S(1)} %pad_maximum_fusion.7), channel_id=1, source_target_pairs={{0,1},{1,2},{2,3},{3,0},{4,5},{5,6},{6,7},{7,4},{8,9},{9,10},{10,1... | collective-permute-start | bytes 73736 | tf_op jit(solution)/shard_map/ppermute | solution.py:23
  10.5 3.3 %collective-permute-start.3 = (f32[4,6,2,128]{3,2,1,0:T(2,128)S(1)}, f32[4,6,2,128]{3,2,1,0:T(2,128)S(1)}, u32[]{:S(2)}, u32[]{:S(2)}) collective-permute-start(f32[4,6,2,128]{3,2,1,0:T(2,128)S(1)} %pad_maximum_fusion.7), channel_id=1, source_target_pairs={{1,0},{2,1},{3,2},{0,3},{5,4},{6,5},{7,6},{4,7},{9,8},{10,9},{11,1... | collective-permute-start | bytes 73736 | tf_op jit(solution)/shard_map/ppermute | solution.py:26
  15.2 48.1 %copy-start.2 = (s32[1,1,12]{2,1,0:T(1,128)S(1)}, s32[1,1,12]{2,1,0:T(1,128)}, u32[]{:S(2)}) copy-start(s32[1,1,12]{2,1,0:T(1,128)} %param.13) | copy-start | bytes 148
  15.3 62.9 %copy-start = (f32[2,2,128]{2,1,0:T(2,128)S(1)}, f32[2,2,128]{2,1,0:T(2,128)}, u32[]{:S(2)}) copy-start(f32[2,2,128]{2,1,0:T(2,128)} %param.11) | copy-start | bytes 6148
  15.3 62.9 %copy-start.1 = (f32[2,2,128]{2,1,0:T(2,128)S(1)}, f32[2,2,128]{2,1,0:T(2,128)}, u32[]{:S(2)}) copy-start(f32[2,2,128]{2,1,0:T(2,128)} %param.12) | copy-start | bytes 6148
  63.6 6.2 %collective-permute-start.4 = (f32[1,2,6,128]{3,2,1,0:T(8,128)S(1)}, f32[1,2,6,128]{3,2,1,0:T(8,128)S(1)}, u32[]{:S(2)}, u32[]{:S(2)}) collective-permute-start(f32[1,2,6,128]{3,2,1,0:T(8,128)S(1)} %get-tuple-element.324), channel_id=1, source_target_pairs={{0,28},{4,0},{8,4},{12,8},{16,12},{20,16},{24,20},{28,24},{1,29},{... | collective-permute-start | bytes 18440 | tf_op jit(solution)/shard_map/ppermute | solution.py:33
  68.4 6.3 %collective-permute-start.5 = (f32[1,2,6,128]{3,2,1,0:T(8,128)S(1)}, f32[1,2,6,128]{3,2,1,0:T(8,128)S(1)}, u32[]{:S(2)}, u32[]{:S(2)}) collective-permute-start(f32[1,2,6,128]{3,2,1,0:T(8,128)S(1)} %get-tuple-element.325), channel_id=1, source_target_pairs={{0,4},{4,8},{8,12},{12,16},{16,20},{20,24},{24,28},{28,0},{1,5},{5... | collective-permute-start | bytes 18440 | tf_op jit(solution)/shard_map/ppermute | solution.py:33
  74.8 1.7 collective-permute-start.6
  75.1 3.0 %collective-permute-start.7 = (f32[1,2,2,128]{3,2,1,0:T(2,128)S(1)}, f32[1,2,2,128]{3,2,1,0:T(2,128)S(1)}, u32[]{:S(2)}, u32[]{:S(2)}) collective-permute-start(f32[1,2,2,128]{3,2,1,0:T(2,128)S(1)} %get-tuple-element.329), channel_id=1, source_target_pairs={{0,1},{1,2},{2,3},{3,0},{4,5},{5,6},{6,7},{7,4},{8,9},{9,10},{10,1... | collective-permute-start | bytes 6152 | tf_op jit(solution)/shard_map/ppermute | solution.py:33
  78.2 6.3 %collective-permute-start.8 = (f32[1,2,2,128]{3,2,1,0:T(2,128)S(1)}, f32[1,2,2,128]{3,2,1,0:T(2,128)S(1)}, u32[]{:S(2)}, u32[]{:S(2)}) collective-permute-start(f32[1,2,2,128]{3,2,1,0:T(2,128)S(1)} %bitcast.107), channel_id=1, source_target_pairs={{0,4},{4,8},{8,12},{12,16},{16,20},{20,24},{24,28},{28,0},{1,5},{5... | collective-permute-start | bytes 6152 | tf_op jit(solution)/shard_map/ppermute | solution.py:23
  78.2 6.3 %collective-permute-start.9 = (f32[1,2,2,128]{3,2,1,0:T(2,128)S(1)}, f32[1,2,2,128]{3,2,1,0:T(2,128)S(1)}, u32[]{:S(2)}, u32[]{:S(2)}) collective-permute-start(f32[1,2,2,128]{3,2,1,0:T(2,128)S(1)} %bitcast.108), channel_id=1, source_target_pairs={{4,0},{8,4},{12,8},{16,12},{20,16},{24,20},{28,24},{0,28},{5,1},{9... | collective-permute-start | bytes 6152 | tf_op jit(solution)/shard_map/ppermute | solution.py:26
  84.5 3.1 %collective-permute-start.10 = (f32[1,6,2,128]{3,2,1,0:T(2,128)S(1)}, f32[1,6,2,128]{3,2,1,0:T(2,128)S(1)}, u32[]{:S(2)}, u32[]{:S(2)}) collective-permute-start(f32[1,6,2,128]{3,2,1,0:T(2,128)S(1)} %pad_maximum_fusion.9), channel_id=1, source_target_pairs={{0,1},{1,2},{2,3},{3,0},{4,5},{5,6},{6,7},{7,4},{8,9},{9,10},{10,1... | collective-permute-start | bytes 18440 | tf_op jit(solution)/shard_map/ppermute | solution.py:23
  84.6 3.1 %collective-permute-start.11 = (f32[1,6,2,128]{3,2,1,0:T(2,128)S(1)}, f32[1,6,2,128]{3,2,1,0:T(2,128)S(1)}, u32[]{:S(2)}, u32[]{:S(2)}) collective-permute-start(f32[1,6,2,128]{3,2,1,0:T(2,128)S(1)} %pad_maximum_fusion.9), channel_id=1, source_target_pairs={{1,0},{2,1},{3,2},{0,3},{5,4},{6,5},{7,6},{4,7},{9,8},{10,9},{11,1... | collective-permute-start | bytes 18440 | tf_op jit(solution)/shard_map/ppermute | solution.py:26
  161.3 6.3 %collective-permute-start.12 = (f32[4,2,6,128]{3,2,1,0:T(8,128)S(1)}, f32[4,2,6,128]{3,2,1,0:T(8,128)S(1)}, u32[]{:S(2)}, u32[]{:S(2)}) collective-permute-start(f32[4,2,6,128]{3,2,1,0:T(8,128)S(1)} %copy.25), channel_id=1, source_target_pairs={{0,28},{4,0},{8,4},{12,8},{16,12},{20,16},{24,20},{28,24},{1,29},{... | collective-permute-start | bytes 73736 | tf_op jit(solution)/shard_map/ppermute | solution.py:33
  166.0 6.6 %collective-permute-start.13 = (f32[4,2,6,128]{3,2,1,0:T(8,128)S(1)}, f32[4,2,6,128]{3,2,1,0:T(8,128)S(1)}, u32[]{:S(2)}, u32[]{:S(2)}) collective-permute-start(f32[4,2,6,128]{3,2,1,0:T(8,128)S(1)} %copy.26), channel_id=1, source_target_pairs={{0,4},{4,8},{8,12},{12,16},{16,20},{20,24},{24,28},{28,0},{1,5},{5... | collective-permute-start | bytes 73736 | tf_op jit(solution)/shard_map/ppermute | solution.py:33
  172.7 1.7 collective-permute-start.14
  173.0 3.1 %collective-permute-start.15 = (f32[4,2,2,128]{3,2,1,0:T(2,128)S(1)}, f32[4,2,2,128]{3,2,1,0:T(2,128)S(1)}, u32[]{:S(2)}, u32[]{:S(2)}) collective-permute-start(f32[4,2,2,128]{3,2,1,0:T(2,128)S(1)} %get-tuple-element.323), channel_id=1, source_target_pairs={{0,1},{1,2},{2,3},{3,0},{4,5},{5,6},{6,7},{7,4},{8,9},{9,10},{10,1... | collective-permute-start | bytes 24584 | tf_op jit(solution)/shard_map/ppermute | solution.py:33
where the time goes:
time: 178 us; the launch traced here: 177 us
  other arithmetic  114 us (64%)
  starting transfers between devices  25.1 us (14%)
  waiting for transfers between devices  22.6 us (13%)
  local copies, waits for them, and re-layouts  11.8 us (7%)
    reduce_max x16, other arithmetic, assign(): peak_score = jnp.max(scores, axis=1, keepdims=True)  20.1 us
    ppermute x8, waiting for transfers between devices, from_behind(): lax.ppermute(shard, axis, [(i, (i + by) % peers) for i in range(peers)])  17.9 us
    reduce_sum x8, other arithmetic, assign(): offsets = -jnp.sum(shares[None] * spread, axis=2)  14.9 us
    reduce_sum x16, other arithmetic, assign(): masses = jnp.sum(shares, axis=0)  13.5 us
    ppermute x4, starting transfers between devices, with_halo(): lax.ppermute(lax.slice_in_dim(block, 0, width, axis=dim), axis, backward)  11.3 us
    reduce_sum x16, other arithmetic, assign(): shares = weights / jnp.sum(weights, axis=1, keepdims=True)  11.1 us
    sub x16, other arithmetic, assign(): spread = points[:, :, None] - chosen[:3, None, :]  11.1 us
    select_n x16, other arithmetic, grid_points(): cell_z = serial % Z  10.8 us
  transfers between devices with their start and end apart: 16, of which 12 were waited for; matrix products, arithmetic and copies ran while one was open for 1% of the time, Pallas kernels for 0%

commit v1 on v0

v1 whole, which is shorter than its diff:
```python
import functools
import math

import jax
import jax.numpy as jnp
from jax import lax
from jax.experimental import pallas as pl
from jax.experimental.pallas import tpu as pltpu
from jax.sharding import PartitionSpec as P

TX = 4
TY = 4
Z = 256

entropy_scale = 0.5
step_rate = 0.5

SCALE = 1.0 / (entropy_scale * math.log(2.0))
DEAD = -1e30
CHUNK = 16
AROUND = [d for d in range(9) if d != 4]
QUADS = [(a, b) for a in range(TX // 2) for b in range(TY // 2)]
NT = (((1,), (1,)), ((), ()))
NN = (((1,), (0,)), ((), ()))


def halves(value):
    high = value.astype(jnp.bfloat16)
    low = (value - high.astype(jnp.float32)).astype(jnp.bfloat16)
    return high, low


def product(pair, high, low, dims):
    rows = pair.shape[0] // 2
    both = lax.dot_general(pair, high, dims, preferred_element_type=jnp.float32)
    rest = lax.dot_general(pair[:rows], low, dims, preferred_element_type=jnp.float32)
    return both[:rows] + both[rows:] + rest


def kernel(
    frac_ref, dual_ref, target_ref, list_ref, count_ref,
    new_ref, shift_ref, disp_ref,
    frac_all, dual_all, mid_all, part_send, part_recv, four_send, four_recv,
    table, base_ref, plain_pair, terms, terms_pair,
    g_high, g_low, gz_high, gz_low, send_sem, recv_sem,
):
    side = frac_ref.shape[1]
    block = frac_ref.shape[3]
    slots = list_ref.shape[2]
    columns = slots * block
    span = 3 * side
    gx, gy = lax.axis_index("gx"), lax.axis_index("gy")
    nx, ny = lax.axis_size("gx"), lax.axis_size("gy")

    def device(d):
        return (lax.rem(gx + d // 3 - 1 + nx, nx), lax.rem(gy + d % 3 - 1 + ny, ny))

    def copy(phase, d, src, dst):
        return pltpu.make_async_remote_copy(
            src_ref=src, dst_ref=dst.at[8 - d],
            send_sem=send_sem.at[phase, d], recv_sem=recv_sem.at[phase, 8 - d],
            device_id=device(d), device_id_type=pl.DeviceIdType.MESH,
        )

    def finish(copies):
        for one in copies:
            one.wait()

    barrier = pltpu.get_barrier_semaphore()
    for d in AROUND:
        pl.semaphore_signal(
            barrier, inc=1, device_id=device(d), device_id_type=pl.DeviceIdType.MESH
        )
    pl.semaphore_wait(barrier, len(AROUND))

    first = [copy(0, d, frac_ref, frac_all) for d in AROUND]
    first += [copy(1, d, dual_ref, dual_all) for d in AROUND]
    for one in first:
        one.start()
    frac_all[4] = frac_ref[...]
    dual_all[4] = dual_ref[...]
    finish(first)

    ids = [list_ref[0, 0, m] for m in range(slots)]
    live = count_ref[0, 0]
    places = []
    for m in range(slots):
        row, col = ids[m] // span, ids[m] % span
        tile_x, tile_y = row // side, col // side
        places.append((tile_x * 3 + tile_y, row % side, col % side))
        at = slice(m * block, (m + 1) * block)
        where = (places[m][1], places[m][2])
        table[0:1, at] = (
            frac_all[places[m][0], 0, where[0], pl.ds(where[1], 1), :] * TX
            + (tile_x - 1).astype(jnp.float32) * TX
        )
        table[1:2, at] = (
            frac_all[places[m][0], 1, where[0], pl.ds(where[1], 1), :] * TY
            + (tile_y - 1).astype(jnp.float32) * TY
        )
        table[2:3, at] = frac_all[places[m][0], 2, where[0], pl.ds(where[1], 1), :] * Z

    def load_duals(source):
        for m in range(slots):
            row = source[places[m][0], places[m][1], pl.ds(places[m][2], 1), :]
            table[3:4, m * block : (m + 1) * block] = jnp.where(m < live, row * SCALE, DEAD)

    load_duals(dual_all)

    serial = lax.broadcasted_iota(jnp.int32, (16, columns), 0)
    kind = serial % 4
    step_x = (serial // 8).astype(jnp.float32) - 0.5
    step_y = (serial // 4 % 2).astype(jnp.float32) - 0.5
    for n, (a, b) in enumerate(QUADS):
        centre_x = (2 * a + 1.0) - table[0:1, :]
        centre_y = (2 * b + 1.0) - table[1:2, :]
        base_ref[n : n + 1, :] = -SCALE * (centre_x * centre_x + centre_y * centre_y)
        plain = jnp.exp2((-2.0 * SCALE) * (step_x * centre_x + step_y * centre_y))
        factor = jnp.where(kind == 1, centre_x + step_x, jnp.where(kind == 2, centre_y + step_y, 1.0))
        with_factor = plain * factor
        terms[n] = with_factor
        high, low = halves(plain)
        plain_pair[n, :16] = high
        plain_pair[n, 16:] = low
        high, low = halves(with_factor)
        terms_pair[n, :16] = high
        terms_pair[n, 16:] = low

    def build(with_moments):
        levels = [base_ref[n : n + 1, :] + table[3:4, :] for n in range(len(QUADS))]

        def chunk(c, carry):
            start = pl.multiple_of(c * CHUNK, CHUNK)
            z = lax.broadcasted_iota(jnp.int32, (CHUNK, columns), 0) + start
            dz = (z.astype(jnp.float32) + 0.5) - table[2:3, :]
            depth = dz * dz * (-SCALE)
            for n in range(len(QUADS)):
                score = depth + levels[n]
                g = jnp.exp2(score - jnp.max(score, axis=1, keepdims=True))
                high, low = halves(g)
                g_high[n, pl.ds(start, CHUNK), :] = high
                g_low[n, pl.ds(start, CHUNK), :] = low
                if with_moments:
                    high, low = halves(g * dz)
                    gz_high[n, pl.ds(start, CHUNK), :] = high
                    gz_low[n, pl.ds(start, CHUNK), :] = low
            return carry

        lax.fori_loop(0, Z // CHUNK, chunk, 0)

    def fold_rows(total):
        eight = total[:8] + total[8:]
        return eight + pltpu.roll(eight, 4, 0)

    shape = (side, side, block)
    inner = lax.broadcasted_iota(jnp.int32, shape, 0) * side + lax.broadcasted_iota(
        jnp.int32, shape, 1
    )

    def place(rows, kind_index, d):
        found = jnp.zeros(shape, jnp.float32)
        for m in range(slots):
            value = rows[kind_index : kind_index + 1, m * block : (m + 1) * block]
            wanted = places[m][1] * side + places[m][2] + (side * side) * (places[m][0] - d)
            found = found + jnp.where(
                inner == wanted, jnp.broadcast_to(value[None], shape), 0.0
            )
        return found

    build(False)
    total = jnp.zeros((16, columns), jnp.float32)
    for n in range(len(QUADS)):
        sums = product(plain_pair[n], g_high[n], g_low[n], NT)
        pair = jnp.concatenate(halves(1.0 / sums), axis=0)
        total = total + terms[n] * product(pair, g_high[n], g_low[n], NN)
    rows = fold_rows(total)
    for d in range(9):
        part_send[d] = place(rows, 0, d)
    second = [copy(2, d, part_send.at[d], part_recv) for d in AROUND]
    for one in second:
        one.start()
    finish(second)
    mass = part_send[4]
    for d in AROUND:
        mass = mass + part_recv[d]
    dual_mid = dual_ref[...] + step_rate * (target_ref[...] - mass)
    mid_all[4] = dual_mid
    third = [copy(3, d, mid_all.at[4], mid_all) for d in AROUND]
    for one in third:
        one.start()
    finish(third)

    load_duals(mid_all)
    build(True)
    total = jnp.zeros((16, columns), jnp.float32)
    is_z = kind == 3
    for n, (a, b) in enumerate(QUADS):
        sums = product(plain_pair[n], g_high[n], g_low[n], NT)
        inverse = 1.0 / sums
        pair = jnp.concatenate(halves(inverse), axis=0)
        masses = product(pair, g_high[n], g_low[n], NN)
        depths = product(pair, gz_high[n], gz_low[n], NN)
        total = total + terms[n] * jnp.where(is_z, depths, masses)
        across = product(terms_pair[n], g_high[n], g_low[n], NT)
        along = product(plain_pair[n], gz_high[n], gz_low[n], NT)
        offset = -inverse * jnp.where(is_z[:, :Z], along, across)
        for r in range(4):
            for c in range(3):
                disp_ref[c, 2 * a + r // 2, 2 * b + r % 2 : 2 * b + r % 2 + 1, :] = offset[
                    4 * r + c + 1 : 4 * r + c + 2, :
                ]
    rows = fold_rows(total)
    for d in range(9):
        for c in range(4):
            four_send[d, c] = place(rows, c, d)
    fourth = [copy(4, d, four_send.at[d], four_recv) for d in AROUND]
    for one in fourth:
        one.start()
    finish(fourth)
    four = four_send[4]
    for d in AROUND:
        four = four + four_recv[d]
    new_ref[...] = dual_mid + step_rate * (target_ref[...] - four[0])
    weight = 1.0 / (four[0] + target_ref[...])
    for c in range(3):
        shift_ref[c] = four[c + 1] * weight


def on_device(site_frac, dual_weight, target_mass, block_list, block_count):
    side = site_frac.shape[1]
    block = site_frac.shape[3]
    columns = block_list.shape[2] * block
    quads = len(QUADS)
    f32, bf16 = jnp.float32, jnp.bfloat16
    vmem = pl.BlockSpec(memory_space=pltpu.VMEM)
    smem = pl.BlockSpec(memory_space=pltpu.SMEM)
    return pl.pallas_call(
        kernel,
        out_shape=(
            jax.ShapeDtypeStruct(dual_weight.shape, f32),
            jax.ShapeDtypeStruct(site_frac.shape, f32),
            jax.ShapeDtypeStruct((3, TX, TY, Z), f32),
        ),
        in_specs=[vmem, vmem, vmem, smem, smem],
        out_specs=(vmem, vmem, vmem),
        scratch_shapes=[
            pltpu.VMEM((9,) + site_frac.shape, f32),
            pltpu.VMEM((9,) + dual_weight.shape, f32),
            pltpu.VMEM((9,) + dual_weight.shape, f32),
            pltpu.VMEM((9, side, side, block), f32),
            pltpu.VMEM((9, side, side, block), f32),
            pltpu.VMEM((9, 4, side, side, block), f32),
            pltpu.VMEM((9, 4, side, side, block), f32),
            pltpu.VMEM((8, columns), f32),
            pltpu.VMEM((8, columns), f32),
            pltpu.VMEM((quads, 32, columns), bf16),
            pltpu.VMEM((quads, 16, columns), f32),
            pltpu.VMEM((quads, 32, columns), bf16),
            pltpu.VMEM((quads, Z, columns), bf16),
            pltpu.VMEM((quads, Z, columns), bf16),
            pltpu.VMEM((quads, Z, columns), bf16),
            pltpu.VMEM((quads, Z, columns), bf16),
            pltpu.SemaphoreType.DMA((5, 9)),
            pltpu.SemaphoreType.DMA((5, 9)),
        ],
        compiler_params=pltpu.CompilerParams(collective_id=0, has_side_effects=True),
        name="transport",
    )(site_frac, dual_weight, target_mass, block_list, block_count)


def solution(mesh):
    in_specs = (
        P(None, "gx", "gy", None),
        P("gx", "gy", None),
        P("gx", "gy", None),
        P("gx", "gy", None),
        P("gx", "gy"),
    )
    out_specs = (P("gx", "gy", None), P(None, "gx", "gy", None), P(None, "gx", "gy", None))
    return jax.shard_map(
        on_device, mesh=mesh, in_specs=in_specs, out_specs=out_specs, check_vma=False
    )
```

time: 178 us -> 51.3 us (0.29)
  other arithmetic: 114 us -> 0 us
  Pallas kernels: 0 us -> 46.5 us
  starting transfers between devices: 25.1 us -> 0 us
  waiting for transfers between devices: 22.6 us -> 0 us
  local copies, waits for them, and re-layouts: 11.8 us -> 3.29 us
    pallas_call x0 -> x1, Pallas kernels: none -> 46.5 us  [on_device(): pl.pallas_call(kernel, out_shape=(jax.ShapeDtypeStruct(dual_weight.shape,...]
    reduce_sum x40 -> x0, other arithmetic: 39.5 us -> none  [the longest x8 14.9 us: assign(): offsets = -jnp.sum(shares[None] * spread, axis=2)]
    ppermute x16 -> x0, starting transfers between devices: 25.1 us -> none  [the longest x4 11.3 us: with_halo(): lax.ppermute(lax.slice_in_dim(block, 0, width, axis=dim), axis, backward)]
    ppermute x16 -> x0, waiting for transfers between devices: 22.6 us -> none  [the longest x8 17.9 us: from_behind(): lax.ppermute(shard, axis, [(i, (i + by) % peers) for i in range(peers)])]
    select_n x33 -> x0, other arithmetic: 22 us -> none  [the longest x16 10.8 us: grid_points(): cell_z = serial % Z]
    reduce_max x16 -> x0, other arithmetic: 20.1 us -> none  [assign(): peak_score = jnp.max(scores, axis=1, keepdims=True)]
    sub x16 -> x0, other arithmetic: 11.1 us -> none  [assign(): spread = points[:, :, None] - chosen[:3, None, :]]
    lt x17 -> x0, other arithmetic: 10.5 us -> none  [the longest x16 10.5 us: on_device(): usable = jnp.arange(slot_count * block_size) // block_size < live_count]
  transfers between devices with their start and end apart: 16 -> 0, of which waited for: 12 -> 0; matrix products, arithmetic and copies ran while one was open for 1% -> 0% of each run, Pallas kernels for 0% -> 0%
where the time goes in v1:
time: 51.3 us; the launch traced here: 51.1 us
  Pallas kernels  46.5 us (91%)
  local copies, waits for them, and re-layouts  3.29 us (6%)
  between operations  1.3 us (3%)
    pallas_call x1, Pallas kernels, on_device(): pl.pallas_call(kernel, out_shape=(jax.ShapeDtypeStruct(dual_weight.shape,...  46.5 us
    unnamed x5, local copies, waits for them, and re-layouts  3.29 us

profile of v1, /device:TPU:0, one launch (start us, length us, event | category | flops | bytes accessed | tf_op | source)
XLA Modules:
  0.0 51.1 jit_solution(12973625567249216968)
XLA Ops:
  1.3 46.5 %transport.1 = (f32[2,2,128]{2,1,0:T(2,128)}, f32[3,2,2,128]{3,2,1,0:T(2,128)}, f32[3,4,4,256]{3,2,1,0:T(4,128)}) custom-call(f32[3,2,2,128]{3,2,1,0:T(2,128)} %frac_ref.1, f32[2,2,128]{2,1,0:T(2,128)} %dual_ref.1, f32[2,2,128]{2,1,0:T(2,128)} %target_ref.1, s32[1,1,12]{2,1,0:T(1,128)} %list_ref.1, s32[1,1]{1,0:T(1,128)S(6)} %copy.11.count_ref), custom_call_target="tpu_custom_call" | custom-call | tf_op jit(solution)/shard_map/transport/pallas_call | solution.py:237
  47.8 0.0 copy-start
  47.8 1.3 %copy.12 = f32[2,2,128]{2,1,0:T(2,128)} copy(f32[2,2,128]{2,1,0:T(2,128)} %get-tuple-element.6) | data formatting | bytes 4096
  49.1 0.0 copy-done
  49.1 0.6 %copy.13 = f32[3,2,2,128]{3,2,1,0:T(2,128)} copy(f32[3,2,2,128]{3,2,1,0:T(2,128)S(1)} %copy-done) | data formatting | bytes 12288
  49.7 1.4 %copy.14 = f32[3,4,4,256]{3,2,1,0:T(4,128)} copy(f32[3,4,4,256]{3,2,1,0:T(4,128)} %get-tuple-element.8) | data formatting | bytes 98304
Async XLA Ops:
  47.8 1.3 %copy-start = (f32[3,2,2,128]{3,2,1,0:T(2,128)S(1)}, f32[3,2,2,128]{3,2,1,0:T(2,128)}, u32[]{:S(2)}) copy-start(f32[3,2,2,128]{3,2,1,0:T(2,128)} %get-tuple-element.7) | copy-start | bytes 18436

commit v2 on v1

v2 whole, which is shorter than its diff:
```python
import functools
import math

import jax
import jax.numpy as jnp
from jax import lax
from jax.experimental import pallas as pl
from jax.experimental.pallas import tpu as pltpu
from jax.sharding import PartitionSpec as P

TX = 4
TY = 4
Z = 256

entropy_scale = 0.5
step_rate = 0.5

SCALE = 1.0 / (entropy_scale * math.log(2.0))
DEAD = -1e30
LIFT = 40.0
HEAD = 2.0**30
UNIT_XY = 8.0
UNIT_Z = float(Z)
CHUNK = 16
AROUND = [d for d in range(9) if d != 4]
GROUPS = TX // 2
ROWS = 2 * TY * 4
NT = (((1,), (1,)), ((), ()))
NN = (((1,), (0,)), ((), ()))


def halves(value):
    high = value.astype(jnp.bfloat16)
    low = (value - high.astype(jnp.float32)).astype(jnp.bfloat16)
    return high, low


def product(pair, high, low, dims):
    rows = pair.shape[0] // 2
    both = lax.dot_general(pair, high, dims, preferred_element_type=jnp.float32)
    rest = lax.dot_general(pair[:rows], low, dims, preferred_element_type=jnp.float32)
    return both[:rows] + both[rows:] + rest


def kernel(
    frac_ref, dual_ref, target_ref, list_ref, count_ref,
    new_ref, shift_ref, disp_ref,
    frac_all, dual_all, target, mid_all, part_send, part_recv, four_send, four_recv,
    list_held, count_held, table, base_ref, plain_rows, plain_pair, terms, terms_pair,
    inverses, g_high, g_low, gz_high, gz_low, disp_held, send_sem, recv_sem, local_sem,
):
    side = frac_ref.shape[1]
    block = frac_ref.shape[3]
    slots = list_ref.shape[2]
    columns = slots * block
    span = 3 * side
    gx, gy = lax.axis_index("gx"), lax.axis_index("gy")
    nx, ny = lax.axis_size("gx"), lax.axis_size("gy")

    def device(d):
        return (lax.rem(gx + d // 3 - 1 + nx, nx), lax.rem(gy + d % 3 - 1 + ny, ny))

    def copy(phase, d, src, dst):
        return pltpu.make_async_remote_copy(
            src_ref=src, dst_ref=dst.at[8 - d],
            send_sem=send_sem.at[phase, d], recv_sem=recv_sem.at[phase, 8 - d],
            device_id=device(d), device_id_type=pl.DeviceIdType.MESH,
        )

    def begin(copies):
        for one in copies:
            one.start()
        return copies

    def finish(copies):
        for one in copies:
            one.wait()

    barrier = pltpu.get_barrier_semaphore()
    for d in AROUND:
        pl.semaphore_signal(
            barrier, inc=1, device_id=device(d), device_id_type=pl.DeviceIdType.MESH
        )
    finish(begin([
        pltpu.make_async_copy(src, dst, local_sem.at[n])
        for n, (src, dst) in enumerate([
            (frac_ref, frac_all.at[4]), (dual_ref, dual_all.at[4]), (target_ref, target),
            (list_ref, list_held), (count_ref, count_held),
        ])
    ]))
    live = count_held[0, 0]
    places = []
    for m in range(slots):
        slot = list_held[0, 0, m]
        row, col = slot // span, slot % span
        places.append(((row // side) * 3 + col // side, row % side, col % side,
                       (row // side - 1).astype(jnp.float32) * TX,
                       (col // side - 1).astype(jnp.float32) * TY))
    pl.semaphore_wait(barrier, len(AROUND))

    finish(begin(
        [copy(0, d, frac_all.at[4], frac_all) for d in AROUND]
        + [copy(1, d, dual_all.at[4], dual_all) for d in AROUND]
    ))

    for m in range(slots):
        tile, row, col, corner_x, corner_y = places[m]
        at = slice(m * block, (m + 1) * block)
        table[0:1, at] = frac_all[tile, 0, row, pl.ds(col, 1), :] * TX + corner_x
        table[1:2, at] = frac_all[tile, 1, row, pl.ds(col, 1), :] * TY + corner_y
        table[2:3, at] = frac_all[tile, 2, row, pl.ds(col, 1), :] * Z

    def load_duals(source):
        for m in range(slots):
            row = source[places[m][0], places[m][1], pl.ds(places[m][2], 1), :]
            table[3:4, m * block : (m + 1) * block] = jnp.where(m < live, row * SCALE, DEAD)

    load_duals(dual_all)

    serial = lax.broadcasted_iota(jnp.int32, (ROWS, columns), 0)
    kind = serial % 4
    step_x = (serial // (4 * TY)).astype(jnp.float32) - 0.5
    step_y = (serial // 4 % TY).astype(jnp.float32) - 0.5 * (TY - 1)

    def centres(n):
        return (2 * n + 1.0) - table[0:1, :], 0.5 * TY - table[1:2, :]

    for n in range(GROUPS):
        centre_x, centre_y = centres(n)
        base_ref[n : n + 1, :] = -SCALE * (centre_x * centre_x + centre_y * centre_y)
        plain = jnp.exp2((-2.0 * SCALE) * (step_x * centre_x + step_y * centre_y))
        plain_rows[n] = plain
        high, low = halves(plain)
        plain_pair[n, :ROWS] = high
        plain_pair[n, ROWS:] = low

    def build(with_moments):
        levels = [base_ref[n : n + 1, :] + table[3:4, :] for n in range(GROUPS)]

        def chunk(c, carry):
            start = pl.multiple_of(c * CHUNK, CHUNK)
            z = lax.broadcasted_iota(jnp.int32, (CHUNK, columns), 0) + start
            dz = (z.astype(jnp.float32) + 0.5) - table[2:3, :]
            depth = dz * dz * (-SCALE)
            for n in range(GROUPS):
                score = depth + levels[n]
                g = jnp.exp2(score - (jnp.max(score, axis=1, keepdims=True) - LIFT))
                high, low = halves(g)
                g_high[n, pl.ds(start, CHUNK), :] = high
                g_low[n, pl.ds(start, CHUNK), :] = low
                if with_moments:
                    high, low = halves(g * (dz * (1.0 / UNIT_Z)))
                    gz_high[n, pl.ds(start, CHUNK), :] = high
                    gz_low[n, pl.ds(start, CHUNK), :] = low
            return carry

        lax.fori_loop(0, Z // CHUNK, chunk, 0, unroll=2)

    def invert(n):
        return HEAD / product(plain_pair[n], g_high[n], g_low[n], NT)

    def fold_rows(total):
        eight = total[:8]
        for r in range(8, ROWS, 8):
            eight = eight + total[r : r + 8]
        return eight + pltpu.roll(eight, 4, 0)

    build(False)
    pairs = [jnp.concatenate(halves(invert(n)), axis=0) for n in range(GROUPS)]
    total = jnp.zeros((ROWS, columns), jnp.float32)
    for n in range(GROUPS):
        total = total + plain_rows[n] * product(pairs[n], g_high[n], g_low[n], NN)
    rows = fold_rows(total) * (1.0 / HEAD)
    shape = (side, side, block)
    inner = lax.broadcasted_iota(jnp.int32, shape, 0) * side + lax.broadcasted_iota(
        jnp.int32, shape, 1
    )
    wanted = [places[m][1] * side + places[m][2] + (side * side) * places[m][0] for m in range(slots)]
    spread = [
        jnp.broadcast_to(rows[0:1, m * block : (m + 1) * block][None], shape) for m in range(slots)
    ]
    for d in range(9):
        found = jnp.zeros(shape, jnp.float32)
        for m in range(slots):
            found = found + jnp.where(inner == wanted[m] - side * side * d, spread[m], 0.0)
        part_send[d] = found
    second = begin([copy(2, d, part_send.at[d], part_recv) for d in AROUND])
    for n in range(GROUPS):
        centre_x, centre_y = centres(n)
        across = (centre_x + step_x) * (1.0 / UNIT_XY)
        aside = (centre_y + step_y) * (1.0 / UNIT_XY)
        factor = jnp.where(kind == 1, across, jnp.where(kind == 2, aside, 1.0))
        with_factor = plain_rows[n] * factor
        terms[n] = with_factor
        high, low = halves(with_factor)
        terms_pair[n, :ROWS] = high
        terms_pair[n, ROWS:] = low
    finish(second)
    mass = part_send[4]
    for d in AROUND:
        mass = mass + part_recv[d]
    dual_mid = dual_all[4] + step_rate * (target[...] - mass)
    mid_all[4] = dual_mid
    finish(begin([copy(3, d, mid_all.at[4], mid_all) for d in AROUND]))

    load_duals(mid_all)
    build(True)
    pairs = []
    for n in range(GROUPS):
        inverse = invert(n)
        inverses[n] = inverse
        pairs.append(jnp.concatenate(halves(inverse), axis=0))
    total = jnp.zeros((ROWS, columns), jnp.float32)
    for n in range(GROUPS):
        masses = product(pairs[n], g_high[n], g_low[n], NN)
        depths = product(pairs[n], gz_high[n], gz_low[n], NN)
        total = total + terms[n] * jnp.where(kind == 3, depths, masses)

    def units(shape):
        which = lax.broadcasted_iota(jnp.int32, shape, 0) % 4
        unit = jnp.where(which == 0, 1.0, jnp.where(which == 3, UNIT_Z, UNIT_XY))
        return unit * (1.0 / HEAD)

    rows = fold_rows(total) * units((8, columns))
    half = lax.broadcasted_iota(jnp.int32, (8, block), 0) // 4
    for d in range(9):
        for v in range(side * side // 2):
            found = jnp.zeros((8, block), jnp.float32)
            for m in range(slots):
                here = half == wanted[m] - (side * side * d + 2 * v)
                found = found + jnp.where(here, rows[:, m * block : (m + 1) * block], 0.0)
            four_send[d, 8 * v : 8 * v + 8, :] = found
    fourth = begin([copy(4, d, four_send.at[d], four_recv) for d in AROUND])
    scale = -units((ROWS, Z))
    is_z = lax.broadcasted_iota(jnp.int32, (ROWS, Z), 0) % 4 == 3
    for n in range(GROUPS):
        across = product(terms_pair[n], g_high[n], g_low[n], NT)
        along = product(plain_pair[n], gz_high[n], gz_low[n], NT)
        offset = (inverses[n] * jnp.where(is_z, along, across)) * scale
        for r in range(2 * TY):
            for c in range(3):
                disp_held[c, 2 * n + r // TY, r % TY : r % TY + 1, :] = offset[
                    4 * r + c + 1 : 4 * r + c + 2, :
                ]
    out = begin([pltpu.make_async_copy(disp_held, disp_ref, local_sem.at[5])])
    finish(fourth)
    four = four_send[4]
    for d in AROUND:
        four = four + four_recv[d]
    for i in range(side * side):
        r, c = i // side, i % side
        goal = target[r, c : c + 1, :]
        found = four[4 * i : 4 * i + 1]
        new_ref[r, c : c + 1, :] = mid_all[4, r, c : c + 1, :] + step_rate * (goal - found)
        weight = 1.0 / (found + goal)
        for k in range(3):
            shift_ref[k, r, c : c + 1, :] = four[4 * i + k + 1 : 4 * i + k + 2] * weight
    finish(out)


def on_device(site_frac, dual_weight, target_mass, block_list, block_count):
    side = site_frac.shape[1]
    block = site_frac.shape[3]
    columns = block_list.shape[2] * block
    f32, bf16, i32 = jnp.float32, jnp.bfloat16, jnp.int32
    vmem = pl.BlockSpec(memory_space=pltpu.VMEM)
    place = pl.BlockSpec(memory_space=pl.ANY)
    return pl.pallas_call(
        kernel,
        out_shape=(
            jax.ShapeDtypeStruct(dual_weight.shape, f32),
            jax.ShapeDtypeStruct(site_frac.shape, f32),
            jax.ShapeDtypeStruct((3, TX, TY, Z), f32),
        ),
        in_specs=[place] * 5,
        out_specs=(vmem, vmem, place),
        scratch_shapes=[
            pltpu.VMEM((9,) + site_frac.shape, f32),
            pltpu.VMEM((9,) + dual_weight.shape, f32),
            pltpu.VMEM(target_mass.shape, f32),
            pltpu.VMEM((9,) + dual_weight.shape, f32),
            pltpu.VMEM((9, side, side, block), f32),
            pltpu.VMEM((9, side, side, block), f32),
            pltpu.VMEM((9, 4 * side * side, block), f32),
            pltpu.VMEM((9, 4 * side * side, block), f32),
            pltpu.SMEM(block_list.shape, i32),
            pltpu.SMEM(block_count.shape, i32),
            pltpu.VMEM((8, columns), f32),
            pltpu.VMEM((8, columns), f32),
            pltpu.VMEM((GROUPS, ROWS, columns), f32),
            pltpu.VMEM((GROUPS, 2 * ROWS, columns), bf16),
            pltpu.VMEM((GROUPS, ROWS, columns), f32),
            pltpu.VMEM((GROUPS, 2 * ROWS, columns), bf16),
            pltpu.VMEM((GROUPS, ROWS, Z), f32),
            pltpu.VMEM((GROUPS, Z, columns), bf16),
            pltpu.VMEM((GROUPS, Z, columns), bf16),
            pltpu.VMEM((GROUPS, Z, columns), bf16),
            pltpu.VMEM((GROUPS, Z, columns), bf16),
            pltpu.VMEM((3, TX, TY, Z), f32),
            pltpu.SemaphoreType.DMA((5, 9)),
            pltpu.SemaphoreType.DMA((5, 9)),
            pltpu.SemaphoreType.DMA((6,)),
        ],
        compiler_params=pltpu.CompilerParams(collective_id=0, has_side_effects=True),
        name="transport",
    )(site_frac, dual_weight, target_mass, block_list, block_count)


def solution(mesh):
    in_specs = (
        P(None, "gx", "gy", None),
        P("gx", "gy", None),
        P("gx", "gy", None),
        P("gx", "gy", None),
        P("gx", "gy"),
    )
    out_specs = (P("gx", "gy", None), P(None, "gx", "gy", None), P(None, "gx", "gy", None))
    return jax.shard_map(
        on_device, mesh=mesh, in_specs=in_specs, out_specs=out_specs, check_vma=False
    )
```

time: 51.3 us -> 37.4 us (0.73)
  Pallas kernels: 46.5 us -> 32.6 us
    pallas_call x1, Pallas kernels: 46.5 us -> 32.6 us  [on_device(): pl.pallas_call(kernel, out_shape=(jax.ShapeDtypeStruct(dual_weight.shape,...]
where the time goes in v2:
time: 37.4 us; the launch traced here: 37.2 us
  Pallas kernels  32.6 us (87%)
  local copies, waits for them, and re-layouts  3.29 us (9%)
  between operations  1.3 us (3%)
    pallas_call x1, Pallas kernels, on_device(): pl.pallas_call(kernel, out_shape=(jax.ShapeDtypeStruct(dual_weight.shape,...  32.6 us
    unnamed x5, local copies, waits for them, and re-layouts  3.29 us

profile of v2, /device:TPU:0, one launch (start us, length us, event | category | flops | bytes accessed | tf_op | source)
XLA Modules:
  0.0 37.2 jit_solution(2952085841385165521)
XLA Ops:
  1.3 32.6 %transport.1 = (f32[2,2,128]{2,1,0:T(2,128)}, f32[3,2,2,128]{3,2,1,0:T(2,128)}, f32[3,4,4,256]{3,2,1,0:T(4,128)}) custom-call(f32[3,2,2,128]{3,2,1,0:T(2,128)} %frac_ref.1, f32[2,2,128]{2,1,0:T(2,128)} %dual_ref.1, f32[2,2,128]{2,1,0:T(2,128)} %target_ref.1, s32[1,1,12]{2,1,0:T(1,128)} %list_ref.1, s32[1,1]{1,0:T(1,128)S(6)} %copy.11.count_ref), custom_call_target="tpu_custom_call" | custom-call | tf_op jit(solution)/shard_map/transport/pallas_call | solution.py:268
  33.9 0.0 copy-start
  33.9 1.3 %copy.12 = f32[2,2,128]{2,1,0:T(2,128)} copy(f32[2,2,128]{2,1,0:T(2,128)} %get-tuple-element.6) | data formatting | bytes 4096
  35.2 0.0 copy-done
  35.2 0.6 %copy.13 = f32[3,2,2,128]{3,2,1,0:T(2,128)} copy(f32[3,2,2,128]{3,2,1,0:T(2,128)S(1)} %copy-done) | data formatting | bytes 12288
  35.7 1.4 %copy.14 = f32[3,4,4,256]{3,2,1,0:T(4,128)} copy(f32[3,4,4,256]{3,2,1,0:T(4,128)} %get-tuple-element.8) | data formatting | bytes 98304
Async XLA Ops:
  33.9 1.3 %copy-start = (f32[3,2,2,128]{3,2,1,0:T(2,128)S(1)}, f32[3,2,2,128]{3,2,1,0:T(2,128)}, u32[]{:S(2)}) copy-start(f32[3,2,2,128]{3,2,1,0:T(2,128)} %get-tuple-element.7) | copy-start | bytes 18436

commit v3 on v2

--- a/solution.py
+++ b/solution.py
@@ -23,6 +23,7 @@
 UNIT_Z = float(Z)
 CHUNK = 16
 AROUND = [d for d in range(9) if d != 4]
+WIDE = [(a, b) for a in range(-2, 3) for b in range(-2, 3) if (a, b) != (0, 0)]
 GROUPS = TX // 2
 ROWS = 2 * TY * 4
 NT = (((1,), (1,)), ((), ()))
@@ -45,9 +46,9 @@
 def kernel(
     frac_ref, dual_ref, target_ref, list_ref, count_ref,
     new_ref, shift_ref, disp_ref,
-    frac_all, dual_all, target, mid_all, part_send, part_recv, four_send, four_recv,
+    frac_all, dual_all, target_all, mid_all, part_send, part_recv, four_send, four_recv,
     list_held, count_held, table, base_ref, plain_rows, plain_pair, terms, terms_pair,
-    inverses, g_high, g_low, gz_high, gz_low, disp_held, send_sem, recv_sem, local_sem,
+    inverses, g_high, g_low, gz_high, gz_low, wide_send, wide_recv, send_sem, recv_sem, local_sem,
 ):
     side = frac_ref.shape[1]
     block = frac_ref.shape[3]
@@ -60,6 +61,19 @@
     def device(d):
         return (lax.rem(gx + d // 3 - 1 + nx, nx), lax.rem(gy + d % 3 - 1 + ny, ny))
 
+    def far(a, b):
+        return (lax.rem(gx + a + nx, nx), lax.rem(gy + b + ny, ny))
+
+    def wide_copy(a, b):
+        here = tuple(pl.ds(max(v, 0), 3 - abs(v)) for v in (a, b))
+        there = tuple(pl.ds(max(-v, 0), 3 - abs(v)) for v in (a, b))
+        e = (a + 2) * 5 + b + 2
+        return pltpu.make_async_remote_copy(
+            src_ref=part_send.at[here], dst_ref=part_recv.at[(24 - e,) + there],
+            send_sem=wide_send.at[e], recv_sem=wide_recv.at[24 - e],
+            device_id=far(a, b), device_id_type=pl.DeviceIdType.MESH,
+        )
+
     def copy(phase, d, src, dst):
         return pltpu.make_async_remote_copy(
             src_ref=src, dst_ref=dst.at[8 - d],
@@ -77,14 +91,14 @@
             one.wait()
 
     barrier = pltpu.get_barrier_semaphore()
-    for d in AROUND:
+    for a, b in WIDE:
         pl.semaphore_signal(
-            barrier, inc=1, device_id=device(d), device_id_type=pl.DeviceIdType.MESH
+            barrier, inc=1, device_id=far(a, b), device_id_type=pl.DeviceIdType.MESH
         )
     finish(begin([
         pltpu.make_async_copy(src, dst, local_sem.at[n])
         for n, (src, dst) in enumerate([
-            (frac_ref, frac_all.at[4]), (dual_ref, dual_all.at[4]), (target_ref, target),
+            (frac_ref, frac_all.at[4]), (dual_ref, dual_all.at[4]), (target_ref, target_all.at[4]),
             (list_ref, list_held), (count_ref, count_held),
         ])
     ]))
@@ -96,12 +110,12 @@
         places.append(((row // side) * 3 + col // side, row % side, col % side,
                        (row // side - 1).astype(jnp.float32) * TX,
                        (col // side - 1).astype(jnp.float32) * TY))
-    pl.semaphore_wait(barrier, len(AROUND))
-
-    finish(begin(
-        [copy(0, d, frac_all.at[4], frac_all) for d in AROUND]
-        + [copy(1, d, dual_all.at[4], dual_all) for d in AROUND]
-    ))
+    pl.semaphore_wait(barrier, len(WIDE))
+
+    first = begin([copy(0, d, frac_all.at[4], frac_all) for d in AROUND])
+    first += begin([copy(1, d, dual_all.at[4], dual_all) for d in AROUND])
+    goals = begin([copy(2, d, target_all.at[4], target_all) for d in AROUND])
+    finish(first)
 
     for m in range(slots):
         tile, row, col, corner_x, corner_y = places[m]
@@ -183,8 +197,8 @@
         found = jnp.zeros(shape, jnp.float32)
         for m in range(slots):
             found = found + jnp.where(inner == wanted[m] - side * side * d, spread[m], 0.0)
-        part_send[d] = found
-    second = begin([copy(2, d, part_send.at[d], part_recv) for d in AROUND])
+        part_send[d // 3, d % 3] = found
+    second = begin([wide_copy(a, b) for a, b in WIDE])
     for n in range(GROUPS):
         centre_x, centre_y = centres(n)
         across = (centre_x + step_x) * (1.0 / UNIT_XY)
@@ -195,13 +209,16 @@
         high, low = halves(with_factor)
         terms_pair[n, :ROWS] = high
         terms_pair[n, ROWS:] = low
+    finish(goals)
     finish(second)
-    mass = part_send[4]
-    for d in AROUND:
-        mass = mass + part_recv[d]
-    dual_mid = dual_all[4] + step_rate * (target[...] - mass)
-    mid_all[4] = dual_mid
-    finish(begin([copy(3, d, mid_all.at[4], mid_all) for d in AROUND]))
+    for i in range(3):
+        for j in range(3):
+            mass = part_send[i, j]
+            for a, b in WIDE:
+                if 0 <= i - max(a, 0) < 3 - abs(a) and 0 <= j - max(b, 0) < 3 - abs(b):
+                    mass = mass + part_recv[(a + 2) * 5 + b + 2, i, j]
+            d = 3 * i + j
+            mid_all[d] = dual_all[d] + step_rate * (target_all[d] - mass)
 
     load_duals(mid_all)
     build(True)
@@ -230,7 +247,7 @@
                 here = half == wanted[m] - (side * side * d + 2 * v)
                 found = found + jnp.where(here, rows[:, m * block : (m + 1) * block], 0.0)
             four_send[d, 8 * v : 8 * v + 8, :] = found
-    fourth = begin([copy(4, d, four_send.at[d], four_recv) for d in AROUND])
+    fourth = begin([copy(3, d, four_send.at[d], four_recv) for d in AROUND])
     scale = -units((ROWS, Z))
     is_z = lax.broadcasted_iota(jnp.int32, (ROWS, Z), 0) % 4 == 3
     for n in range(GROUPS):
@@ -239,23 +256,21 @@
         offset = (inverses[n] * jnp.where(is_z, along, across)) * scale
         for r in range(2 * TY):
             for c in range(3):
-                disp_held[c, 2 * n + r // TY, r % TY : r % TY + 1, :] = offset[
+                disp_ref[c, 2 * n + r // TY, r % TY : r % TY + 1, :] = offset[
                     4 * r + c + 1 : 4 * r + c + 2, :
                 ]
-    out = begin([pltpu.make_async_copy(disp_held, disp_ref, local_sem.at[5])])
     finish(fourth)
     four = four_send[4]
     for d in AROUND:
         four = four + four_recv[d]
     for i in range(side * side):
         r, c = i // side, i % side
-        goal = target[r, c : c + 1, :]
+        goal = target_all[4, r, c : c + 1, :]
         found = four[4 * i : 4 * i + 1]
         new_ref[r, c : c + 1, :] = mid_all[4, r, c : c + 1, :] + step_rate * (goal - found)
         weight = 1.0 / (found + goal)
         for k in range(3):
             shift_ref[k, r, c : c + 1, :] = four[4 * i + k + 1 : 4 * i + k + 2] * weight
-    finish(out)
 
 
 def on_device(site_frac, dual_weight, target_mass, block_list, block_count):
@@ -268,19 +283,19 @@
     return pl.pallas_call(
         kernel,
         out_shape=(
-            jax.ShapeDtypeStruct(dual_weight.shape, f32),
-            jax.ShapeDtypeStruct(site_frac.shape, f32),
-            jax.ShapeDtypeStruct((3, TX, TY, Z), f32),
+            pltpu.VMEM(dual_weight.shape, f32),
+            pltpu.VMEM(site_frac.shape, f32),
+            pltpu.VMEM((3, TX, TY, Z), f32),
         ),
         in_specs=[place] * 5,
-        out_specs=(vmem, vmem, place),
+        out_specs=(vmem, vmem, vmem),
         scratch_shapes=[
             pltpu.VMEM((9,) + site_frac.shape, f32),
             pltpu.VMEM((9,) + dual_weight.shape, f32),
-            pltpu.VMEM(target_mass.shape, f32),
+            pltpu.VMEM((9,) + target_mass.shape, f32),
             pltpu.VMEM((9,) + dual_weight.shape, f32),
-            pltpu.VMEM((9, side, side, block), f32),
-            pltpu.VMEM((9, side, side, block), f32),
+            pltpu.VMEM((3, 3, side, side, block), f32),
+            pltpu.VMEM((25, 3, 3, side, side, block), f32),
             pltpu.VMEM((9, 4 * side * side, block), f32),
             pltpu.VMEM((9, 4 * side * side, block), f32),
             pltpu.SMEM(block_list.shape, i32),
@@ -296,10 +311,11 @@
             pltpu.VMEM((GROUPS, Z, columns), bf16),
             pltpu.VMEM((GROUPS, Z, columns), bf16),
             pltpu.VMEM((GROUPS, Z, columns), bf16),
-            pltpu.VMEM((3, TX, TY, Z), f32),
-            pltpu.SemaphoreType.DMA((5, 9)),
-            pltpu.SemaphoreType.DMA((5, 9)),
-            pltpu.SemaphoreType.DMA((6,)),
+            pltpu.SemaphoreType.DMA((25,)),
+            pltpu.SemaphoreType.DMA((25,)),
+            pltpu.SemaphoreType.DMA((4, 9)),
+            pltpu.SemaphoreType.DMA((4, 9)),
+            pltpu.SemaphoreType.DMA((5,)),
         ],
         compiler_params=pltpu.CompilerParams(collective_id=0, has_side_effects=True),
         name="transport",

time: 37.4 us -> 31.6 us (0.84)
  Pallas kernels: 32.6 us -> 28.3 us
  local copies, waits for them, and re-layouts: 3.29 us -> 1.79 us
    pallas_call x1, Pallas kernels: 32.6 us -> 28.3 us  [on_device(): pl.pallas_call(kernel, out_shape=(pltpu.VMEM(dual_weight.shape, f32), plt...]
    unnamed x5 -> x3, local copies, waits for them, and re-layouts: 3.29 us -> 1.79 us
where the time goes in v3:
time: 31.6 us; the launch traced here: 31.4 us
  Pallas kernels  28.3 us (90%)
  local copies, waits for them, and re-layouts  1.79 us (6%)
  between operations  1.29 us (4%)
    pallas_call x1, Pallas kernels, on_device(): pl.pallas_call(kernel, out_shape=(pltpu.VMEM(dual_weight.shape, f32), plt...  28.3 us
    unnamed x3, local copies, waits for them, and re-layouts  1.79 us

profile of v3, /device:TPU:0, one launch (start us, length us, event | category | flops | bytes accessed | tf_op | source)
XLA Modules:
  0.0 31.4 jit_solution(1062449076079080521)
XLA Ops:
  1.3 28.3 %transport.1 = (f32[2,2,128]{2,1,0:T(2,128)S(1)}, f32[3,2,2,128]{3,2,1,0:T(2,128)S(1)}, f32[3,4,4,256]{3,2,1,0:T(4,128)S(1)}) custom-call(f32[3,2,2,128]{3,2,1,0:T(2,128)} %frac_ref.1, f32[2,2,128]{2,1,0:T(2,128)} %dual_ref.1, f32[2,2,128]{2,1,0:T(2,128)} %target_ref.1, s32[1,1,12]{2,1,0:T(1,128)} %list_ref.1, s32[1,1]{1,0:T(1,128)S(6)} %copy.14.count_ref), custom_call_target="tpu_custom_call" | custom-call | tf_op jit(solution)/shard_map/transport/pallas_call | solution.py:283
  29.6 0.6 %copy.11 = f32[2,2,128]{2,1,0:T(2,128)} copy(f32[2,2,128]{2,1,0:T(2,128)S(1)} %get-tuple-element.3) | data formatting | bytes 4096
  30.2 0.6 %copy.12 = f32[3,2,2,128]{3,2,1,0:T(2,128)} copy(f32[3,2,2,128]{3,2,1,0:T(2,128)S(1)} %get-tuple-element.4) | data formatting | bytes 12288
  30.8 0.6 %copy.13 = f32[3,4,4,256]{3,2,1,0:T(4,128)} copy(f32[3,4,4,256]{3,2,1,0:T(4,128)S(1)} %get-tuple-element.5) | data formatting | bytes 98304
